TPU v7x, 128 devices: a whole 4x4x4 slice. The times are simulated.
128 devices in a mesh: scan: 16 (over z_lo, x, core), tgt: 8 (over y, z_hi).
Axes of the slice: x: 4, y: 4, z: 4 (z_hi: 2, z_lo: 2; z = z_hi * 2 + z_lo), core: 2. Of those that a mesh axis runs over, the one named last changes fastest.
Arguments:
- series: bfloat16 [96, 1200, 8192], P('scan', None, 'tgt'), as said below
- seed_index: int32 [512], replicated, may hold values from 0 to 8191
Outputs:
- affinity: bfloat16 [8192, 8192], P('tgt', 'scan')
Inputs may be any that keep to these rules, and one draw needn't show every extreme that they name: No grayordinate's series is constant over the frames of a scan.
All inputs are finite; a program needn't handle non-finite values.
Results may differ from a plain program's by a relative error of at most 0.0034.
Values may be sent and summed in bfloat16 or wider, within the bound.
A program may use at most 128 MiB of HBM per device.

v0:
```python
import jax
import jax.numpy as jnp
from jax import lax
from jax.sharding import PartitionSpec as P

epsilon = 1e-06
clip_level = 0.95
capacity = 96


def fisher_sum(correl):
    clipped = jnp.clip(correl, -clip_level, clip_level)
    above = jnp.prod(1.0 + clipped, axis=0)
    below = jnp.prod(1.0 - clipped, axis=0)
    return 0.5 * jnp.log(above / below)


def normalize_columns(profile):
    center = jnp.mean(profile, axis=0)
    deviate = profile - center
    spread = jnp.mean(deviate * deviate, axis=0)
    return (deviate * lax.rsqrt(spread + epsilon)).astype(jnp.bfloat16)


def body(series, seed_index):
    frame_count = series.shape[1]
    local_width = series.shape[2]
    seed_count = seed_index.shape[0]
    tgt_size = lax.axis_size("tgt")
    scan_size = lax.axis_size("scan")
    whole_width = local_width * tgt_size
    me = lax.axis_index("tgt")
    owner = seed_index // local_width
    local_seed = seed_index - owner * local_width
    owned = owner[:, None] == jnp.arange(tgt_size)[None, :]
    before = jnp.cumsum(owned.astype(jnp.int32), axis=0)
    count = before[-1]
    rank = jnp.sum(jnp.where(owned, before, 0), axis=1) - 1
    values = series.astype(jnp.float32)
    center = jnp.mean(values, axis=1, keepdims=True)
    deviate = values - center
    spread = jnp.mean(deviate * deviate, axis=1, keepdims=True)
    standard = (deviate * lax.rsqrt(spread + epsilon)).astype(jnp.bfloat16)

    def correlate(seed_cols):
        correl = jnp.einsum("sfk,sfg->skg", seed_cols, standard, preferred_element_type=jnp.float32)
        return fisher_sum(correl / frame_count)

    def packed():
        mine = (owner == me)[:, None] & (rank[:, None] == jnp.arange(capacity)[None, :])
        column = jnp.sum(jnp.where(mine, local_seed[:, None] + 1, 0), axis=0) - 1
        pick = (jnp.arange(local_width)[:, None] == column[None, :]).astype(jnp.bfloat16)
        picked = jnp.einsum(
            "sfg,gk->sfk", standard, pick, preferred_element_type=jnp.float32
        ).astype(jnp.bfloat16)
        seed_cols = lax.all_gather(picked, "tgt", axis=2, tiled=True)
        return jnp.take(correlate(seed_cols), owner * capacity + rank, axis=0)

    def general():
        inside = owner == me
        picked = jnp.take(standard, local_seed, axis=2)
        picked = jnp.where(inside[None, None, :], picked, jnp.zeros_like(picked))
        return correlate(lax.psum(picked, "tgt"))

    running = lax.cond(jnp.max(count) <= capacity, packed, general)
    part = lax.psum_scatter(running, "scan", scatter_dimension=1, tiled=True)
    row_prof = lax.all_gather(normalize_columns(part), "scan", axis=1, tiled=True)
    col_width = whole_width // scan_size
    spot = lax.axis_index("scan") * col_width
    start = spot % local_width
    col_prof = lax.dynamic_slice_in_dim(row_prof, start, col_width, 1)
    col_prof = jnp.where(spot // local_width == me, col_prof, jnp.zeros_like(col_prof))
    col_prof = lax.psum(col_prof, "tgt")
    product = jnp.dot(row_prof.T, col_prof, preferred_element_type=jnp.float32)
    return jnp.tanh(product / seed_count).astype(jnp.bfloat16)


def solution(mesh):
    in_specs = (P("scan", None, "tgt"), P())
    out_specs = P("tgt", "scan")
    return jax.shard_map(body, mesh=mesh, in_specs=in_specs, out_specs=out_specs, check_vma=False)
```

profile of v0, /device:TPU:0, one launch (start us, length us, event | category | flops | bytes accessed | tf_op | source)
XLA Modules:
  0.0 424.0 jit_solution(14349586945426796302)
XLA Ops:
  7.4 0.7 multiply_subtract_fusion
  8.1 1.1 reduce-window.6
  9.2 0.2 slice_reduce_fusion
  9.5 0.1 add_bitcast_fusion
  9.5 8.8 %convert_reduce_fusion = f32[6,1024]{1,0:T(8,128)S(1)} fusion(bf16[6,1200,1024]{2,1,0:T(8,128)(2,1)} %param.4), kind=kLoop, calls=%fused_computation.32 | loop fusion | flops 14739456 | bytes 14770176 | tf_op jit(solution)/shard_map/reduce_sum | solution.py:40
  18.3 9.0 %fusion.7 = f32[6,1024]{1,0:T(8,128)S(1)} fusion(bf16[6,1200,1024]{2,1,0:T(8,128)(2,1)} %param.4, f32[6,1024]{1,0:T(8,128)S(1)} %broadcast_multiply_fusion), kind=kLoop, calls=%fused_computation.35 | loop fusion | flops 29485056 | bytes 14794752 | tf_op jit(solution)/shard_map/reduce_sum | solution.py:42
  27.4 11.7 %fusion.8 = bf16[6,1200,1024]{2,1,0:T(8,128)(2,1)} fusion(bf16[6,1200,1024]{2,1,0:T(8,128)(2,1)} %param.4, f32[6,1024]{1,0:T(8,128)S(1)} %add_rsqrt_fusion, f32[6,1024]{1,0:T(8,128)S(1)} %broadcast_multiply_fusion), kind=kLoop, calls=%fused_computation.36 | loop fusion | flops 29491200 | bytes 29540352 | tf_op jit(solution)/shard_map/convert_element_type | solution.py:43
  39.1 0.7 slice_reduce_fusion.1
  40.5 185.9 %conditional.1 = (f32[512,1024]{1,0:T(8,128)S(1)}) conditional(s32[]{:T(128)} %convert_element_type.28, (s32[]{:T(128)}, s32[512]{0:T(512)S(1)}, s32[512]{0:T(512)S(1)}, bf16[6,1200,1024]{2,1,0:T(8,128)(2,1)}) %tuple.11, (s32[512]{0:T(512)S(1)}, s32[512,8]{0,1:T(8,128)S(1)}, s32[512,8]{0,1:T(8,128)S(1)}, s32[512]{0:T(512)S(1)}, s32[]{:T(128)}, ...), branch_computations={%region_5.9_spmd, %region_9.14_spmd} | conditional | flops 12770038784 | bytes 150587424 | solution.py:65
  40.7 0.0 all-gather.3.cloned.1.call-start
  40.8 0.1 select_reduce_fusion
  41.0 10.8 %fusion = bf16[6,1200,96]{1,2,0:T(8,128)(2,1)} fusion(bf16[6,1200,1024]{2,1,0:T(8,128)(2,1)} %get-tuple-element.49, s32[96]{0:T(128)S(1)} %broadcast_add_fusion.1), kind=kOutput, calls=%fused_computation.16 | convolution fusion | flops 1416367104 | bytes 16128384 | tf_op jit(solution)/shard_map/cond/branch_1_fun/sfg,gk->sfk/dot_general | solution.py:53
  51.8 0.0 all-gather.3.cloned.1.call-update
  51.9 142.9 %all-gather.3.cloned.1.call-done = bf16[6,1200,768]{1,2,0:T(8,128)(2,1)} async-done(((bf16[6,1200,96]{1,2,0:T(8,128)(2,1)}), bf16[6,1200,768]{1,2,0:T(8,128)(2,1)}) %all-gather.3.cloned.1.call-update) | async-done | bytes 11059216 | tf_op jit(solution)/shard_map/cond/branch_1_fun/all_gather | solution.py:56
  194.7 23.5 %subtract_reduce_fusion.1 = (f32[768,1024]{1,0:T(8,128)}, f32[768,1024]{1,0:T(8,128)}) fusion(bf16[6,1200,768]{1,2,0:T(8,128)(2,1)} %all-gather.3.cloned.1.call-done, bf16[6,1200,1024]{2,1,0:T(8,128)(2,1)} %get-tuple-element.49), kind=kOutput, calls=%fused_computation.11 | convolution fusion | flops 11351359488 | bytes 32096256 | tf_op jit(solution)/shard_map/cond/branch_1_fun/sfk,sfg->skg/dot_general | solution.py:46
  218.2 3.7 log_multiply_fusion.1
  221.9 2.7 gather_fusion.1
  224.6 1.8 broadcast_select_fusion
  226.4 0.0 reduce-scatter.4.cloned.1.call-start
  226.4 1.9 copy.18
  228.3 0.0 reduce-scatter.4.cloned.1.call-update
  228.3 0.0 all-gather.5.cloned.1.call-start
  228.4 61.9 %reduce-scatter.4.cloned.1.call-done = f32[64,512]{1,0:T(8,128)} async-done(((f32[1024,512]{1,0:T(8,128)}), f32[64,512]{1,0:T(8,128)}) %reduce-scatter.4.cloned.1.call-update) | async-done | bytes 131088
  290.3 1.0 bitcast_reduce_fusion
  291.3 1.1 multiply_reduce_fusion
  292.4 1.6 multiply_convert_fusion
  294.0 0.0 all-gather.5.cloned.1.call-update
  294.1 0.0 all-reduce.5.cloned.1.call-start
  294.1 31.1 %all-gather.5.cloned.1.call-done = bf16[512,1024]{0,1:T(8,128)(2,1)} async-done(((bf16[512,64]{0,1:T(8,128)(2,1)}), bf16[512,1024]{0,1:T(8,128)(2,1)}) %all-gather.5.cloned.1.call-update) | async-done | bytes 1048592 | tf_op jit(solution)/shard_map/all_gather | solution.py:67
  325.2 1.9 dynamic-slice_select_fusion
  327.2 0.0 all-reduce.5.cloned.1.call-update
  327.2 86.1 %all-reduce.5.cloned.1.call-done = bf16[512,512]{0,1:T(8,128)(2,1)} async-done(((bf16[512,512]{0,1:T(8,128)(2,1)}), bf16[512,512]{0,1:T(8,128)(2,1)}) %all-reduce.5.cloned.1.call-update) | async-done | bytes 524304 | tf_op jit(solution)/shard_map/psum | solution.py:73
  413.3 3.1 tanh_convert_fusion
  (14 shorter events, 0.1 us)
Async XLA Ops:
  40.7 154.0 %all-gather.3.cloned.1.call-start = ((), (), s32[]{:S(2)}) async-start(), calls=%async_computation.2 | async-start | bytes 13271040 | tf_op jit(solution)/shard_map/cond/branch_1_fun/all_gather | solution.py:56
  226.4 63.9 %reduce-scatter.4.cloned.1.call-start = ((), (), s32[]{:S(2)}) async-start(), calls=%async_computation.5 | async-start | bytes 2228224
  228.3 96.9 %all-gather.5.cloned.1.call-start = ((), (), s32[]{:S(2)}) async-start(), calls=%async_computation.3 | async-start | bytes 1114112 | tf_op jit(solution)/shard_map/all_gather | solution.py:67
  294.1 119.2 %all-reduce.5.cloned.1.call-start = ((), (), s32[]{:S(2)}) async-start(), calls=%async_computation.4 | async-start | bytes 1048576 | tf_op jit(solution)/shard_map/psum | solution.py:73
Sparse Core Ops, SparseCore 0:
  52.0 142.6 all-gather.2
Sparse Core Ops, SparseCore 1:
  229.2 61.0 reduce-scatter.3
  294.1 31.0 all-gather.4
  327.6 85.7 all-reduce.4
where the time goes:
time: 424 us
  waiting for transfers between devices  322 us (76%)
  other arithmetic  43.5 us (10%)
  matrix products  37.4 us (9%)
  between operations  15.8 us (4%)
  local copies, waits for them, and re-layouts  4.82 us (1%)
    all_gather x1, waiting for transfers between devices, packed(): seed_cols = lax.all_gather(picked, 'tgt', axis=2, tiled=True)  143 us
    psum x1, waiting for transfers between devices, body(): col_prof = lax.psum(col_prof, 'tgt')  86.1 us
    unnamed x4, waiting for transfers between devices  61.9 us
    all_gather x1, waiting for transfers between devices, body(): lax.all_gather(normalize_columns(part), 'scan', axis=1, tiled=True)  31.1 us
    dot_general x1, matrix products, correlate(): jnp.einsum('sfk,sfg->skg', seed_cols, standard, preferred_element_type=jn...  23.5 us
    convert_element_type x1, other arithmetic, body(): standard = (deviate * lax.rsqrt(spread + epsilon)).astype(jnp.bfloat16)  11.7 us
    dot_general x1, matrix products, packed(): jnp.einsum('sfg,gk->sfk', standard, pick, preferred_element_type=jnp.floa...  10.8 us
    reduce_sum x1, other arithmetic, body(): spread = jnp.mean(deviate * deviate, axis=1, keepdims=True)  9.04 us
  transfers between devices with their start and end apart: 4, of which 4 were waited for; matrix products, arithmetic and copies ran while one was open for 0% of the time, Pallas kernels for 0%

commit v1 on v0

--- a/solution.py
+++ b/solution.py
@@ -53,7 +53,9 @@
         picked = jnp.einsum(
             "sfg,gk->sfk", standard, pick, preferred_element_type=jnp.float32
         ).astype(jnp.bfloat16)
-        seed_cols = lax.all_gather(picked, "tgt", axis=2, tiled=True)
+        seed_cols = jnp.concatenate(
+            lax.all_to_all(jnp.stack([picked] * lax.axis_size("tgt")), "tgt", 0, 0), axis=2
+        )
         return jnp.take(correlate(seed_cols), owner * capacity + rank, axis=0)
 
     def general():

time: 424 us -> 467 us (1.10)
  waiting for transfers between devices: 322 us -> 342 us
  local copies, waits for them, and re-layouts: 4.82 us -> 20.7 us
  starting transfers between devices: 0.17 us -> 8 us
    all_to_all x0 -> x1, waiting for transfers between devices: none -> 161 us  [packed(): lax.all_to_all(jnp.stack([picked] * lax.axis_size('tgt')), 'tgt', 0, 0)]
    all_gather x1 -> x0, waiting for transfers between devices: 143 us -> none  [packed(): seed_cols = lax.all_gather(picked, 'tgt', axis=2, tiled=True)]
    reshape x0 -> x1, local copies, waits for them, and re-layouts: none -> 10.1 us  [packed(): jnp.concatenate(lax.all_to_all(jnp.stack([picked] * lax.axis_size('tgt'))...]
    all_to_all x0 -> x1, starting transfers between devices: none -> 7.86 us  [packed(): lax.all_to_all(jnp.stack([picked] * lax.axis_size('tgt')), 'tgt', 0, 0)]
    another operation x2 -> x3, local copies, waits for them, and re-layouts: 0.01 us -> 5.81 us  [the longest x1 5.8 us: packed(): jnp.stack([picked] * lax.axis_size('tgt'))]
where the time goes in v1:
time: 467 us
  waiting for transfers between devices  342 us (73%)
  other arithmetic  43.5 us (9%)
  matrix products  36.2 us (8%)
  local copies, waits for them, and re-layouts  20.7 us (4%)
  between operations  15.8 us (3%)
  starting transfers between devices  8 us (2%)
    all_to_all x1, waiting for transfers between devices, packed(): lax.all_to_all(jnp.stack([picked] * lax.axis_size('tgt')), 'tgt', 0, 0)  161 us
    psum x1, waiting for transfers between devices, body(): col_prof = lax.psum(col_prof, 'tgt')  86.1 us
    unnamed x4, waiting for transfers between devices  63.9 us
    all_gather x1, waiting for transfers between devices, body(): lax.all_gather(normalize_columns(part), 'scan', axis=1, tiled=True)  31.1 us
    dot_general x1, matrix products, correlate(): jnp.einsum('sfk,sfg->skg', seed_cols, standard, preferred_element_type=jn...  23.5 us
    convert_element_type x1, other arithmetic, body(): standard = (deviate * lax.rsqrt(spread + epsilon)).astype(jnp.bfloat16)  11.7 us
    reshape x1, local copies, waits for them, and re-layouts, packed(): jnp.concatenate(lax.all_to_all(jnp.stack([picked] * lax.axis_size('tgt'))...  10.1 us
    dot_general x1, matrix products, packed(): jnp.einsum('sfg,gk->sfk', standard, pick, preferred_element_type=jnp.floa...  9.65 us
  transfers between devices with their start and end apart: 4, of which 4 were waited for; matrix products, arithmetic and copies ran while one was open for 0% of the time, Pallas kernels for 0%

profile of v1, /device:TPU:0, one launch (start us, length us, event | category | flops | bytes accessed | tf_op | source)
XLA Modules:
  0.0 466.9 jit_solution(17587957959107857154)
XLA Ops:
  7.4 0.7 multiply_subtract_fusion
  8.1 1.1 reduce-window.6
  9.2 0.2 slice_reduce_fusion
  9.5 0.1 add_bitcast_fusion
  9.5 8.8 %convert_reduce_fusion = f32[6,1024]{1,0:T(8,128)S(1)} fusion(bf16[6,1200,1024]{2,1,0:T(8,128)(2,1)} %param.4), kind=kLoop, calls=%fused_computation.32 | loop fusion | flops 14739456 | bytes 14770176 | tf_op jit(solution)/shard_map/reduce_sum | solution.py:40
  18.3 9.0 %fusion.7 = f32[6,1024]{1,0:T(8,128)S(1)} fusion(bf16[6,1200,1024]{2,1,0:T(8,128)(2,1)} %param.4, f32[6,1024]{1,0:T(8,128)S(1)} %broadcast_multiply_fusion), kind=kLoop, calls=%fused_computation.35 | loop fusion | flops 29485056 | bytes 14794752 | tf_op jit(solution)/shard_map/reduce_sum | solution.py:42
  27.4 11.7 %fusion.8 = bf16[6,1200,1024]{2,1,0:T(8,128)(2,1)} fusion(bf16[6,1200,1024]{2,1,0:T(8,128)(2,1)} %param.4, f32[6,1024]{1,0:T(8,128)S(1)} %add_rsqrt_fusion, f32[6,1024]{1,0:T(8,128)S(1)} %broadcast_multiply_fusion), kind=kLoop, calls=%fused_computation.36 | loop fusion | flops 29491200 | bytes 29540352 | tf_op jit(solution)/shard_map/convert_element_type | solution.py:43
  39.1 0.7 slice_reduce_fusion.1
  40.5 226.9 %conditional.1 = (f32[512,1024]{1,0:T(8,128)S(1)}) conditional(s32[]{:T(128)} %convert_element_type.28, (s32[]{:T(128)}, s32[512]{0:T(512)S(1)}, s32[512]{0:T(512)S(1)}, bf16[6,1200,1024]{2,1,0:T(8,128)(2,1)}) %tuple.11, (s32[512]{0:T(512)S(1)}, s32[512,8]{0,1:T(8,128)S(1)}, s32[512,8]{0,1:T(8,128)S(1)}, s32[512]{0:T(512)S(1)}, s32[]{:T(128)}, ...), branch_computations={%region_5.9_spmd, %region_9.14_spmd} | conditional | flops 12770038784 | bytes 150587424 | solution.py:67
  40.8 0.1 select_reduce_fusion
  40.9 9.7 %fusion = bf16[6,1200,96]{1,2,0:T(8,128)(2,1)S(1)} fusion(bf16[6,1200,1024]{2,1,0:T(8,128)(2,1)} %get-tuple-element.49, s32[96]{0:T(128)S(1)} %broadcast_add_fusion.1), kind=kOutput, calls=%fused_computation.16 | convolution fusion | flops 1416367104 | bytes 16128384 | tf_op jit(solution)/shard_map/cond/branch_1_fun/sfg,gk->sfk/dot_general | solution.py:53
  50.6 5.8 %stack.0 = bf16[8,6,1200,96]{2,3,1,0:T(8,128)(2,1)} broadcast(bf16[6,1200,96]{1,2,0:T(8,128)(2,1)S(1)} %fusion), dimensions={1,2,3} | broadcast | bytes 12441600 | tf_op jit(solution)/shard_map/cond/branch_1_fun/stack | solution.py:57
  56.4 7.9 %all-to-all-start = ((bf16[8,6,1200,96]{2,3,1,0:T(8,128)(2,1)}), bf16[8,6,1200,96]{2,3,1,0:T(8,128)(2,1)}, u32[]{:S(2)}, u32[]{:S(2)}) async-start(bf16[8,6,1200,96]{2,3,1,0:T(8,128)(2,1)} %stack.0), calls=%async_computation | async-start | bytes 23592960 | tf_op jit(solution)/shard_map/cond/branch_1_fun/all_to_all | solution.py:57
  64.3 161.4 %all-to-all-done = bf16[8,6,1200,96]{2,3,1,0:T(8,128)(2,1)} async-done(((bf16[8,6,1200,96]{2,3,1,0:T(8,128)(2,1)}), bf16[8,6,1200,96]{2,3,1,0:T(8,128)(2,1)}, u32[]{:S(2)}, u32[]{:S(2)}) %all-to-all-start) | async-done | bytes 11059232 | tf_op jit(solution)/shard_map/cond/branch_1_fun/all_to_all | solution.py:57
  225.7 10.1 %copy.22 = bf16[6,1200,8,96]{1,3,2,0:T(8,128)(2,1)} copy(bf16[6,1200,8,96]{1,3,0,2:T(8,128)(2,1)} %bitcast.3) | data formatting | bytes 22118400 | tf_op jit(solution)/shard_map/cond/branch_1_fun/reshape | solution.py:56
  235.7 23.5 %subtract_reduce_fusion.1 = (f32[768,1024]{1,0:T(8,128)}, f32[768,1024]{1,0:T(8,128)}) fusion(bf16[6,1200,768]{1,2,0:T(8,128)(2,1)} %bitcast.29, bf16[6,1200,1024]{2,1,0:T(8,128)(2,1)} %get-tuple-element.49), kind=kOutput, calls=%fused_computation.11 | convolution fusion | flops 11351359488 | bytes 32096256 | tf_op jit(solution)/shard_map/cond/branch_1_fun/sfk,sfg->skg/dot_general | solution.py:46
  259.2 3.7 log_multiply_fusion.1
  262.9 2.7 gather_fusion
  265.6 1.8 broadcast_select_fusion
  267.4 0.0 reduce-scatter.4.cloned.1.call-start
  267.5 1.9 copy.27
  269.4 0.0 reduce-scatter.4.cloned.1.call-update
  269.4 0.0 all-gather.2.cloned.1.call-start
  269.4 63.8 %reduce-scatter.4.cloned.1.call-done = f32[64,512]{1,0:T(8,128)} async-done(((f32[1024,512]{1,0:T(8,128)}), f32[64,512]{1,0:T(8,128)}) %reduce-scatter.4.cloned.1.call-update) | async-done | bytes 131088
  333.2 1.0 bitcast_reduce_fusion
  334.3 1.1 multiply_reduce_fusion
  335.4 1.6 multiply_convert_fusion
  337.0 0.0 all-gather.2.cloned.1.call-update
  337.0 0.0 all-reduce.5.cloned.1.call-start
  337.1 31.1 %all-gather.2.cloned.1.call-done = bf16[512,1024]{0,1:T(8,128)(2,1)} async-done(((bf16[512,64]{0,1:T(8,128)(2,1)}), bf16[512,1024]{0,1:T(8,128)(2,1)}) %all-gather.2.cloned.1.call-update) | async-done | bytes 1048592 | tf_op jit(solution)/shard_map/all_gather | solution.py:69
  368.2 1.9 dynamic-slice_select_fusion
  370.1 0.0 all-reduce.5.cloned.1.call-update
  370.1 86.1 %all-reduce.5.cloned.1.call-done = bf16[512,512]{0,1:T(8,128)(2,1)} async-done(((bf16[512,512]{0,1:T(8,128)(2,1)}), bf16[512,512]{0,1:T(8,128)(2,1)}) %all-reduce.5.cloned.1.call-update) | async-done | bytes 524304 | tf_op jit(solution)/shard_map/psum | solution.py:75
  456.3 3.1 tanh_convert_fusion
  (14 shorter events, 0.1 us)
Async XLA Ops:
  56.4 169.3 %all-to-all-start = ((bf16[8,6,1200,96]{2,3,1,0:T(8,128)(2,1)}), bf16[8,6,1200,96]{2,3,1,0:T(8,128)(2,1)}, u32[]{:S(2)}, u32[]{:S(2)}) async-start(bf16[8,6,1200,96]{2,3,1,0:T(8,128)(2,1)} %stack.0), calls=%async_computation | async-start | bytes 23592960 | tf_op jit(solution)/shard_map/cond/branch_1_fun/all_to_all | solution.py:57
  267.4 65.8 %reduce-scatter.4.cloned.1.call-start = ((), (), s32[]{:S(2)}) async-start(), calls=%async_computation.5 | async-start | bytes 2228224
  269.4 98.8 %all-gather.2.cloned.1.call-start = ((), (), s32[]{:S(2)}) async-start(), calls=%async_computation.3 | async-start | bytes 1114112 | tf_op jit(solution)/shard_map/all_gather | solution.py:69
  337.0 119.2 %all-reduce.5.cloned.1.call-start = ((), (), s32[]{:S(2)}) async-start(), calls=%async_computation.4 | async-start | bytes 1048576 | tf_op jit(solution)/shard_map/psum | solution.py:75
Sparse Core Ops, SparseCore 1:
  270.3 62.9 reduce-scatter.3
  337.1 31.0 all-gather.1
  370.5 85.7 all-reduce.4
